TPU v7x, 32 devices: a whole 2x2x4 slice. The times are simulated.
32 devices in a mesh: rows: 8 (over z, x), scales: 4 (over y, core).
Axes of the slice: x: 2, y: 2, z: 4, core: 2. Of those that a mesh axis runs over, the one named last changes fastest.
Arguments:
- image_now: float32 [256, 8192], P(('rows', 'scales')), may hold values from 0.1 to 4
- gradient: float32 [256, 8192], P(('rows', 'scales')), may hold values from -140 to 140
- hessian_weight: float32 [256, 8192], P(('rows', 'scales')), may hold values from 0.1 to 10
- psf_tiles: float32 [32, 256], P(('rows', 'scales')), may hold values from -0.5 to 1.7
- facet_of_row: int32 [256], P(('rows', 'scales')), may hold values from 0 to 31, never falling along the last dimension, each value on 1 to 32 neighbouring positions
- tile_slot: int32 [32], replicated, may hold values from 0 to 31, each once
- thresholds: float32 [4], replicated, may hold values from 0.2 to 2
Outputs:
- new_image: float32 [256, 8192], P(('rows', 'scales'))
Inputs may be any that keep to these rules, and one draw needn't show every extreme that they name: `facet_of_row`: facet numbers never fall along the rows; every facet covers 1 to 32 rows, and some facet exactly 32. `tile_slot`: each facet's tile stands in a different row of psf_tiles, and every row holds one.
All inputs are finite; a program needn't handle non-finite values.
Results may differ from a plain program's by a relative error of at most 0.0001.
Values sent between devices are 32-bit elements; how exact they have to be, the bound alone decides.
A program may use at most 64 MiB of HBM per device.

v0:
```python
import jax
import jax.numpy as jnp
from jax import lax
from jax.sharding import PartitionSpec as P

TILE = 16
SUBITERS = 2
SPLINE_EDGE = 0.0625
SPLINE_NEAR = 0.25
SPLINE_MID = 0.375


def padded_2(cells, sides, width):
    for axis, dim in sides:
        count = lax.axis_size(axis)
        ends = count - 1
        head = lax.slice_in_dim(cells, 0, width, axis=dim)
        tail = lax.slice_in_dim(cells, cells.shape[dim] - width, cells.shape[dim], axis=dim)
        cells = jnp.concatenate(
            [
                lax.ppermute(tail, axis, [(i, (i + 1) % count) for i in range(ends)]),
                cells,
                lax.ppermute(head, axis, [((i + 1) % count, i) for i in range(ends)]),
            ],
            axis=dim,
        )
    return cells


def along_columns(source, spacing):
    length = source.shape[1]
    padded = jnp.pad(source, ((0, 0), (2 * spacing, 2 * spacing)))
    outer_pair = padded[:, 0:length] + padded[:, 4 * spacing : 4 * spacing + length]
    inner_pair = (
        padded[:, spacing : spacing + length] + padded[:, 3 * spacing : 3 * spacing + length]
    )
    return SPLINE_EDGE * outer_pair + SPLINE_NEAR * inner_pair + SPLINE_MID * source


def rows_traced(source, spacing, reach):
    length = source.shape[0]
    padded = jnp.pad(source, ((reach, reach), (0, 0)))

    def shifted_rows(offset):
        return lax.dynamic_slice_in_dim(padded, reach + offset, length, 0)

    outer_pair = shifted_rows(-2 * spacing) + shifted_rows(2 * spacing)
    inner_pair = shifted_rows(-spacing) + shifted_rows(spacing)
    return SPLINE_EDGE * outer_pair + SPLINE_NEAR * inner_pair + SPLINE_MID * source


def widen_band(source):
    half_tile = TILE // 2
    extended = padded_2(source, ((("rows", "scales"), 0),), half_tile)
    return jnp.pad(extended, ((0, 0), (half_tile, half_tile)))


def forward_blur(source, weights):
    band_rows, columns = source.shape
    padded = widen_band(source)

    def forward_add_tap_row(tap_row, summed):
        shifted = lax.dynamic_slice_in_dim(padded, tap_row, band_rows, 0)
        tap_weights = lax.dynamic_index_in_dim(weights, tap_row, 1, keepdims=False)
        for column in range(TILE):
            summed = (
                summed + tap_weights[:, column : column + 1] * shifted[:, column : column + columns]
            )
        return summed

    return lax.fori_loop(0, TILE, forward_add_tap_row, jnp.zeros((band_rows, columns), jnp.float32))


def adjoint_blur(source, wide_weights):
    band_rows, columns = source.shape
    half_tile = TILE // 2
    padded = widen_band(source)

    def adjoint_add_tap_row(tap_row, summed):
        offset = 2 * half_tile - tap_row
        shifted = lax.dynamic_slice_in_dim(padded, offset, band_rows, 0)
        weight_rows = lax.dynamic_slice_in_dim(wide_weights, offset, band_rows, 0)
        tap_weights = lax.dynamic_index_in_dim(weight_rows, tap_row, 1, keepdims=False)
        for column in range(TILE):
            offset_col = 2 * half_tile - column
            summed = (
                summed
                + tap_weights[:, column : column + 1]
                * shifted[:, offset_col : offset_col + columns]
            )
        return summed

    return lax.fori_loop(0, TILE, adjoint_add_tap_row, jnp.zeros((band_rows, columns), jnp.float32))


def body(image_now, gradient, hessian_weight, psf_tiles, facet_of_row, tile_slot, thresholds):
    band_rows, columns = image_now.shape
    half_tile = TILE // 2
    scale_count = lax.axis_size("scales")
    scale_index = lax.axis_index("scales")
    facet_ids = jnp.arange(tile_slot.shape[0], dtype=jnp.int32)
    slot_rows = jnp.sum(
        jnp.where(facet_of_row[:, None] == facet_ids[None, :], tile_slot[None, :], 0), axis=1
    )
    tiles_in = lax.all_gather(psf_tiles, ("rows", "scales"), axis=0, tiled=True)
    length = tiles_in.shape[0]
    onehot = (slot_rows[:, None] == jnp.arange(length, dtype=jnp.int32)[None, :]).astype(
        jnp.float32
    )
    flat_rows = jnp.dot(
        onehot, tiles_in, precision=lax.Precision.HIGHEST, preferred_element_type=jnp.float32
    )
    wide_rows = padded_2(flat_rows, ((("rows", "scales"), 0),), half_tile)
    weights = flat_rows.reshape(band_rows, TILE, TILE)
    wide_weights = wide_rows.reshape(band_rows + 2 * half_tile, TILE, TILE)
    level_gain = jnp.sum(jnp.where(jnp.arange(scale_count) == scale_index, thresholds, 0.0))
    reach = 2**scale_count

    def column_level(depth, plane):
        return rows_traced(plane, jnp.left_shift(jnp.int32(1), depth), reach)

    current = image_now
    for sweep in range(SUBITERS):
        change = current - image_now
        pushed = hessian_weight * forward_blur(change, weights)
        descent = gradient + adjoint_blur(pushed, wide_weights)
        blurred = forward_blur(descent, weights)
        totals = lax.psum(
            (jnp.sum(descent * descent), jnp.sum(hessian_weight * blurred * blurred)),
            ("rows", "scales"),
        )
        step_size = totals[0] / totals[1]
        trial = current - step_size * descent
        stripe = lax.all_gather(trial, "scales", axis=0, tiled=True)
        smooth = stripe
        lower = jnp.zeros_like(stripe)
        upper = jnp.zeros_like(stripe)
        for depth in range(scale_count):
            smoother = along_columns(smooth, 2**depth)
            lower = jnp.where(scale_index == depth, smooth, lower)
            upper = jnp.where(scale_index == depth, smoother, upper)
            smooth = smoother
        limit = step_size * level_gain
        lower_cols, upper_cols = (
            lax.all_to_all(lower, "rows", split_axis=1, concat_axis=0, tiled=True),
            lax.all_to_all(upper, "rows", split_axis=1, concat_axis=0, tiled=True),
        )
        lower_cols = lax.fori_loop(0, scale_index, column_level, lower_cols)
        upper_cols = lax.fori_loop(0, scale_index + 1, column_level, upper_cols)
        detail = lower_cols - upper_cols
        kept = (
            detail
            - jnp.clip(detail, -limit, limit)
            + jnp.where(scale_index == scale_count - 1, upper_cols, 0.0)
        )
        contribution = lax.all_to_all(kept, "rows", split_axis=0, concat_axis=1, tiled=True)
        current = lax.psum_scatter(contribution, "scales", scatter_dimension=0, tiled=True)
    return current


def solution(mesh):
    in_specs = (
        P(("rows", "scales"), None),
        P(("rows", "scales"), None),
        P(("rows", "scales"), None),
        P(("rows", "scales"), None),
        P(("rows", "scales")),
        P(),
        P(),
    )
    out_specs = P(("rows", "scales"), None)
    return jax.shard_map(body, mesh=mesh, in_specs=in_specs, out_specs=out_specs, check_vma=False)
```

profile of v0, /device:TPU:0, one launch (start us, length us, event | category | flops | bytes accessed | tf_op | source)
XLA Modules:
  0.0 672.7 jit_solution(16924233468898300590)
XLA Ops:
  7.6 2.4 collective-permute-start.2
  12.2 45.4 %all-gather = f32[32,1,256]{2,1,0:T(1,128)S(1)} all-gather(f32[1,1,256]{2,1,0:T(1,128)} %bitcast.79), channel_id=1, replica_groups=mesh['rows'=8,'scales'=4] {'rows','scales'}, dimensions={0}, use_global_device_ids=true | all-gather | bytes 33792 | tf_op jit(solution)/shard_map/all_gather | solution.py:105
  58.2 27.8 %while.146 = (s32[]{:T(128)}, f32[8,8192]{1,0:T(8,128)S(1)}, f32[8,16,16]{2,0,1:T(8,128)S(1)}, f32[24,8208]{1,0:T(8,128)S(1)}, s32[]{:T(128)}, /*index=5*/s32[]{...) while((s32[]{:T(128)}, f32[8,8192]{1,0:T(8,128)S(1)}, ...), condition=%wide.region_2.3_spmd.clone, body=%wide.region_1.2_spmd.clone.sunk | while | flops 2162706 | bytes 4721599 | solution.py:71
  89.7 3.0 collective-permute-start
  94.0 2.5 collective-permute-done.1
  97.0 29.6 %while.147 = (s32[]{:T(128)}, f32[8,8192]{1,0:T(8,128)S(1)}, f32[24,16,16]{2,0,1:T(8,128)S(1)}, f32[24,8208]{1,0:T(8,128)S(1)}, s32[]{:T(128)}, /*index=5*/s32[]...) while((s32[]{:T(128)}, f32[8,8192]{1,0:T(8,128)S(1)}, ...), condition=%wide.region_4.5_spmd.clone, body=%wide.region_3.4_spmd.clone.sunk | while | flops 2162713 | bytes 4721729 | solution.py:93
  127.3 4.3 collective-permute-start.6
  135.3 27.8 %while.148 = (s32[]{:T(128)}, f32[8,8192]{1,0:T(8,128)S(1)}, f32[8,16,16]{2,0,1:T(8,128)S(1)}, f32[24,8208]{1,0:T(8,128)S(1)}, s32[]{:T(128)}, /*index=5*/s32[]{...) while((s32[]{:T(128)}, f32[8,8192]{1,0:T(8,128)S(1)}, ...), condition=%wide.region_8.9_spmd.clone, body=%wide.region_7.8_spmd.clone.sunk | while | flops 2162706 | bytes 4721599 | solution.py:71
  163.9 42.4 %all-reduce.19 = (f32[]{:T(128)}, f32[]{:T(128)}) all-reduce(f32[]{:T(128)} %get-tuple-element.1221, f32[]{:T(128)} %fusion.137), channel_id=1, replica_groups=mesh['rows'=8,'scales'=4] {'rows','scales'}, use_global_device_ids=true, to_apply=%region_6.7 | all-reduce | flops 2 | bytes 16 | tf_op jit(solution)/shard_map/psum | solution.py:128
  208.5 17.4 %all-gather.4.cloned.1.call-done = f32[32,8192]{1,0:T(8,128)} async-done(((f32[8,8192]{1,0:T(8,128)}), f32[32,8192]{1,0:T(8,128)}) %all-gather.4.cloned.1.call-update) | async-done | bytes 1048592 | tf_op jit(solution)/shard_map/all_gather | solution.py:134
  225.8 4.2 multiply_add_fusion.5
  236.8 5.5 all-to-all-start.1
  243.4 25.1 %all-to-all-done.1 = f32[32,8,1024]{2,0,1:T(8,128)S(1)} async-done(((f32[32,8,1024]{2,0,1:T(8,128)}), f32[32,8,1024]{2,0,1:T(8,128)S(1)}, u32[]{:S(2)}, u32[]{:S(2)}) %all-to-all-start.1) | async-done | bytes 1048608 | tf_op jit(solution)/shard_map/all_to_all | solution.py:146
  268.5 3.8 all-to-all-start
  274.4 23.8 %all-to-all-done = f32[32,8,1024]{2,0,1:T(8,128)S(1)} async-done(((f32[32,8,1024]{2,0,1:T(8,128)}), f32[32,8,1024]{2,0,1:T(8,128)S(1)}, u32[]{:S(2)}, u32[]{:S(2)}) %all-to-all-start) | async-done | bytes 1048608 | tf_op jit(solution)/shard_map/all_to_all | solution.py:145
  298.5 30.1 %all_to_all.114 = f32[8,32,1024]{2,1,0:T(8,128)S(1)} all-to-all(f32[8,32,1024]{2,1,0:T(8,128)S(1)} %bitcast.72), channel_id=1, replica_groups=mesh['rows'=8,'scales'=4] {'rows'}, dimensions={0} | all-to-all | bytes 2097152 | tf_op jit(solution)/shard_map/all_to_all | solution.py:156
  329.9 24.7 %reduce-scatter.3.cloned.1.call-done = f32[8,8192]{1,0:T(8,128)} async-done(((f32[32,8192]{1,0:T(8,128)}), f32[8,8192]{1,0:T(8,128)}) %reduce-scatter.3.cloned.1.call-update) | async-done | bytes 262160 | tf_op jit(solution)/shard_map/reduce_scatter | solution.py:157
  358.5 2.4 collective-permute-done.9
  361.2 27.8 %while.149 = (s32[]{:T(128)}, f32[8,8192]{1,0:T(8,128)S(1)}, f32[8,16,16]{2,0,1:T(8,128)S(1)}, f32[24,8208]{1,0:T(8,128)S(1)}, s32[]{:T(128)}, /*index=5*/s32[]{...) while((s32[]{:T(128)}, f32[8,8192]{1,0:T(8,128)S(1)}, ...), condition=%wide.region_18.19_spmd.clone, body=%wide.region_17.18_spmd.clone.sunk | while | flops 2162706 | bytes 4721599 | solution.py:71
  389.0 6.7 collective-permute-start.10
  399.4 29.6 %while.150 = (s32[]{:T(128)}, f32[8,8192]{1,0:T(8,128)S(1)}, f32[24,16,16]{2,0,1:T(8,128)S(1)}, f32[24,8208]{1,0:T(8,128)S(1)}, s32[]{:T(128)}, /*index=5*/s32[]...) while((s32[]{:T(128)}, f32[8,8192]{1,0:T(8,128)S(1)}, ...), condition=%wide.region_20.21_spmd.clone, body=%wide.region_19.20_spmd.clone.sunk | while | flops 2162713 | bytes 4721729 | solution.py:93
  429.6 8.0 %collective-permute-start.12 = (f32[8,8192]{1,0:T(8,128)S(1)}, f32[8,8192]{1,0:T(8,128)S(1)}, u32[]{:S(2)}, u32[]{:S(2)}) collective-permute-start(f32[8,8192]{1,0:T(8,128)S(1)} %get-tuple-element.1218), channel_id=1, source_target_pairs={{0,1},{1,2},{2,3},{3,4},{4,5},{5,6},{6,7},{7,8},{8,9},{9,10},{10,1... | collective-permute-start | bytes 786440 | tf_op jit(solution)/shard_map/ppermute | solution.py:21
  441.4 27.8 %while.151 = (s32[]{:T(128)}, f32[8,8192]{1,0:T(8,128)S(1)}, f32[8,16,16]{2,0,1:T(8,128)S(1)}, f32[24,8208]{1,0:T(8,128)S(1)}, s32[]{:T(128)}, /*index=5*/s32[]{...) while((s32[]{:T(128)}, f32[8,8192]{1,0:T(8,128)S(1)}, ...), condition=%wide.region_24.25_spmd.clone, body=%wide.region_23.24_spmd.clone.sunk | while | flops 2162706 | bytes 4721599 | solution.py:71
  470.0 47.3 %all-reduce.18 = (f32[]{:T(128)}, f32[]{:T(128)}) all-reduce(f32[]{:T(128)} %get-tuple-element.1217, f32[]{:T(128)} %fusion.138), channel_id=1, replica_groups=mesh['rows'=8,'scales'=4] {'rows','scales'}, use_global_device_ids=true, to_apply=%region_22.23 | all-reduce | flops 2 | bytes 16 | tf_op jit(solution)/shard_map/psum | solution.py:128
  519.4 18.3 %all-gather.6.cloned.1.call-done = f32[32,8192]{1,0:T(8,128)} async-done(((f32[8,8192]{1,0:T(8,128)}), f32[32,8192]{1,0:T(8,128)}) %all-gather.6.cloned.1.call-update) | async-done | bytes 1048592 | tf_op jit(solution)/shard_map/all_gather | solution.py:134
  537.6 4.2 multiply_add_fusion.2
  548.6 5.5 all-to-all-start.4
  555.2 25.1 %all-to-all-done.4 = f32[32,8,1024]{2,0,1:T(8,128)S(1)} async-done(((f32[32,8,1024]{2,0,1:T(8,128)}), f32[32,8,1024]{2,0,1:T(8,128)S(1)}, u32[]{:S(2)}, u32[]{:S(2)}) %all-to-all-start.4) | async-done | bytes 1048608 | tf_op jit(solution)/shard_map/all_to_all | solution.py:146
  580.3 3.6 all-to-all-start.3
  585.4 24.4 %all-to-all-done.3 = f32[32,8,1024]{2,0,1:T(8,128)S(1)} async-done(((f32[32,8,1024]{2,0,1:T(8,128)}), f32[32,8,1024]{2,0,1:T(8,128)S(1)}, u32[]{:S(2)}, u32[]{:S(2)}) %all-to-all-start.3) | async-done | bytes 1048608 | tf_op jit(solution)/shard_map/all_to_all | solution.py:145
  610.2 30.1 %all_to_all.115 = f32[8,32,1024]{2,1,0:T(8,128)S(1)} all-to-all(f32[8,32,1024]{2,1,0:T(8,128)S(1)} %bitcast.71), channel_id=1, replica_groups=mesh['rows'=8,'scales'=4] {'rows'}, dimensions={0} | all-to-all | bytes 2097152 | tf_op jit(solution)/shard_map/all_to_all | solution.py:156
  641.4 24.8 %reduce-scatter.5.cloned.1.call-done = f32[8,8192]{1,0:T(8,128)} async-done(((f32[32,8192]{1,0:T(8,128)}), f32[8,8192]{1,0:T(8,128)}) %reduce-scatter.5.cloned.1.call-update) | async-done | bytes 262160 | tf_op jit(solution)/shard_map/reduce_scatter | solution.py:157
  (383 shorter events, 218.1 us)
Async XLA Ops:
  6.5 219.3 %all-gather.4.cloned.1.call-start = ((), (), s32[]{:S(2)}) async-start(), calls=%async_computation.8 | async-start | bytes 1310720 | tf_op jit(solution)/shard_map/all_gather | solution.py:134
  7.6 50.3 %collective-permute-start.2 = (f32[8,8192]{1,0:T(8,128)S(1)}, f32[8,8192]{1,0:T(8,128)S(1)}, u32[]{:S(2)}, u32[]{:S(2)}) collective-permute-start(f32[8,8192]{1,0:T(8,128)S(1)} %sub.46), channel_id=1, source_target_pairs={{0,1},{1,2},{2,3},{3,4},{4,5},{5,6},{6,7},{7,8},{8,9},{9,10},{10,1... | collective-permute-start | bytes 786440 | tf_op jit(solution)/shard_map/ppermute | solution.py:21
  10.0 47.9 %collective-permute-start.3 = (f32[8,8192]{1,0:T(8,128)S(1)}, f32[8,8192]{1,0:T(8,128)S(1)}, u32[]{:S(2)}, u32[]{:S(2)}) collective-permute-start(f32[8,8192]{1,0:T(8,128)S(1)} %sub.46), channel_id=1, source_target_pairs={{1,0},{2,1},{3,2},{4,3},{5,4},{6,5},{7,6},{8,7},{9,8},{10,9},{11,1... | collective-permute-start | bytes 786440 | tf_op jit(solution)/shard_map/ppermute | solution.py:23
  58.2 27.8 %copy-start = (f32[8,8192]{1,0:T(8,128)S(1)}, f32[8,8192]{1,0:T(8,128)}, u32[]{:S(2)}) copy-start(f32[8,8192]{1,0:T(8,128)} %param.29) | copy-start | bytes 786436
  86.1 10.6 %collective-permute-start.4 = (f32[8,8192]{1,0:T(8,128)S(1)}, f32[8,8192]{1,0:T(8,128)S(1)}, u32[]{:S(2)}, u32[]{:S(2)}) collective-permute-start(f32[8,8192]{1,0:T(8,128)S(1)} %mul.2942), channel_id=1, source_target_pairs={{0,1},{1,2},{2,3},{3,4},{4,5},{5,6},{6,7},{7,8},{8,9},{9,10},{10,1... | collective-permute-start | bytes 786440 | tf_op jit(solution)/shard_map/ppermute | solution.py:21
  88.4 8.4 %collective-permute-start.5 = (f32[8,8192]{1,0:T(8,128)S(1)}, f32[8,8192]{1,0:T(8,128)S(1)}, u32[]{:S(2)}, u32[]{:S(2)}) collective-permute-start(f32[8,8192]{1,0:T(8,128)S(1)} %mul.2942), channel_id=1, source_target_pairs={{1,0},{2,1},{3,2},{4,3},{5,4},{6,5},{7,6},{8,7},{9,8},{10,9},{11,1... | collective-permute-start | bytes 786440 | tf_op jit(solution)/shard_map/ppermute | solution.py:23
  89.7 4.4 collective-permute-start
  92.7 3.8 collective-permute-start.1
  97.0 29.6 %copy-start.5 = (f32[8,8192]{1,0:T(8,128)S(1)}, f32[8,8192]{1,0:T(8,128)}, u32[]{:S(2)}) copy-start(f32[8,8192]{1,0:T(8,128)} %param.28) | copy-start | bytes 786436
  127.3 5.6 collective-permute-start.6
  131.6 3.4 collective-permute-start.7
  135.3 72.4 %copy-start.1 = (f32[8,8192]{1,0:T(8,128)S(1)}, f32[8,8192]{1,0:T(8,128)}, u32[]{:S(2)}) copy-start(f32[8,8192]{1,0:T(8,128)} %param.27) | copy-start | bytes 786436
  230.0 1.2 copy-start.2
  236.8 31.7 %all-to-all-start.1 = ((f32[32,8,1024]{2,0,1:T(8,128)}), f32[32,8,1024]{2,0,1:T(8,128)S(1)}, u32[]{:S(2)}, u32[]{:S(2)}) async-start(f32[32,8,1024]{2,0,1:T(8,128)} %bitcast.50), calls=%async_computation.1 | async-start | bytes 2097152 | tf_op jit(solution)/shard_map/all_to_all | solution.py:146
  268.5 3.8 copy-start.6
  268.5 29.7 %all-to-all-start = ((f32[32,8,1024]{2,0,1:T(8,128)}), f32[32,8,1024]{2,0,1:T(8,128)S(1)}, u32[]{:S(2)}, u32[]{:S(2)}) async-start(f32[32,8,1024]{2,0,1:T(8,128)} %bitcast.68), calls=%async_computation | async-start | bytes 2097152 | tf_op jit(solution)/shard_map/all_to_all | solution.py:145
  272.3 82.3 %reduce-scatter.3.cloned.1.call-start = ((), (), s32[]{:S(2)}) async-start(), calls=%async_computation.9 | async-start | bytes 1310720 | tf_op jit(solution)/shard_map/reduce_scatter | solution.py:157
  329.8 207.8 %all-gather.6.cloned.1.call-start = ((), (), s32[]{:S(2)}) async-start(), calls=%async_computation.10 | async-start | bytes 1310720 | tf_op jit(solution)/shard_map/all_gather | solution.py:134
  355.6 2.9 collective-permute-start.8
  357.2 3.7 collective-permute-start.9
  389.0 8.2 %collective-permute-start.10 = (f32[8,8192]{1,0:T(8,128)S(1)}, f32[8,8192]{1,0:T(8,128)S(1)}, u32[]{:S(2)}, u32[]{:S(2)}) collective-permute-start(f32[8,8192]{1,0:T(8,128)S(1)} %mul.2961), channel_id=1, source_target_pairs={{0,1},{1,2},{2,3},{3,4},{4,5},{5,6},{6,7},{7,8},{8,9},{9,10},{10,1... | collective-permute-start | bytes 786440 | tf_op jit(solution)/shard_map/ppermute | solution.py:21
  395.7 3.4 collective-permute-start.11
  429.6 9.4 %collective-permute-start.12 = (f32[8,8192]{1,0:T(8,128)S(1)}, f32[8,8192]{1,0:T(8,128)S(1)}, u32[]{:S(2)}, u32[]{:S(2)}) collective-permute-start(f32[8,8192]{1,0:T(8,128)S(1)} %get-tuple-element.1218), channel_id=1, source_target_pairs={{0,1},{1,2},{2,3},{3,4},{4,5},{5,6},{6,7},{7,8},{8,9},{9,10},{10,1... | collective-permute-start | bytes 786440 | tf_op jit(solution)/shard_map/ppermute | solution.py:21
  437.7 3.4 collective-permute-start.13
  441.4 77.2 %copy-start.4 = (f32[8,8192]{1,0:T(8,128)S(1)}, f32[8,8192]{1,0:T(8,128)}, u32[]{:S(2)}) copy-start(f32[8,8192]{1,0:T(8,128)} %reduce-scatter.3.cloned.1.call-done) | copy-start | bytes 786436
  541.8 1.2 copy-start.3
  548.6 31.7 %all-to-all-start.4 = ((f32[32,8,1024]{2,0,1:T(8,128)}), f32[32,8,1024]{2,0,1:T(8,128)S(1)}, u32[]{:S(2)}, u32[]{:S(2)}) async-start(f32[32,8,1024]{2,0,1:T(8,128)} %bitcast.48), calls=%async_computation.5 | async-start | bytes 2097152 | tf_op jit(solution)/shard_map/all_to_all | solution.py:146
  580.3 29.6 %all-to-all-start.3 = ((f32[32,8,1024]{2,0,1:T(8,128)}), f32[32,8,1024]{2,0,1:T(8,128)S(1)}, u32[]{:S(2)}, u32[]{:S(2)}) async-start(f32[32,8,1024]{2,0,1:T(8,128)} %bitcast.49), calls=%async_computation.4 | async-start | bytes 2097152 | tf_op jit(solution)/shard_map/all_to_all | solution.py:145
  583.9 82.3 %reduce-scatter.5.cloned.1.call-start = ((), (), s32[]{:S(2)}) async-start(), calls=%async_computation.11 | async-start | bytes 1310720 | tf_op jit(solution)/shard_map/reduce_scatter | solution.py:157
Sparse Core Ops, SparseCore 0:
  208.6 17.2 all-gather.3
  329.9 24.6 reduce-scatter.2
  519.5 18.0 all-gather.5
  641.5 24.6 reduce-scatter.4
where the time goes:
time: 674 us; the launch traced here: 673 us
  blocking collectives  196 us (29%)
  waiting for transfers between devices  195 us (29%)
  other arithmetic  156 us (23%)
  starting transfers between devices  56.1 us (8%)
  local copies, waits for them, and re-layouts  49.5 us (7%)
  between operations  17.6 us (3%)
    psum x2, blocking collectives, body(): lax.psum((jnp.sum(descent * descent), jnp.sum(hessian_weight * blurred *...  89.8 us
    add x64, other arithmetic, forward_add_tap_row(): summed + tap_weights[:, column:column + 1] * shifted[:, column:column + c...  81 us
    all_to_all x2, blocking collectives, body(): lax.all_to_all(kept, 'rows', split_axis=0, concat_axis=1, tiled=True)  60.3 us
    all_to_all x2, waiting for transfers between devices, body(): lax.all_to_all(upper, 'rows', split_axis=1, concat_axis=0, tiled=True)  50.2 us
    reduce_scatter x2, waiting for transfers between devices, body(): lax.psum_scatter(contribution, 'scales', scatter_dimension=0, tiled=True)  49.5 us
    all_to_all x2, waiting for transfers between devices, body(): lax.all_to_all(lower, 'rows', split_axis=1, concat_axis=0, tiled=True)  48.3 us
    all_gather x1, blocking collectives, body(): tiles_in = lax.all_gather(psf_tiles, ('rows', 'scales'), axis=0, tiled=True)  45.4 us
    add x32, other arithmetic, adjoint_add_tap_row(): summed + tap_weights[:, column:column + 1] * shifted[:, offset_col:offset...  43.6 us
  transfers between devices with their start and end apart: 22, of which 13 were waited for; matrix products, arithmetic and copies ran while one was open for 1% of the time, Pallas kernels for 0%

commit v1 on v0

--- a/solution.py
+++ b/solution.py
@@ -153,7 +153,10 @@
             - jnp.clip(detail, -limit, limit)
             + jnp.where(scale_index == scale_count - 1, upper_cols, 0.0)
         )
-        contribution = lax.all_to_all(kept, "rows", split_axis=0, concat_axis=1, tiled=True)
+        contribution = jnp.concatenate(
+            lax.all_to_all(jnp.stack(jnp.split(kept, lax.axis_size("rows"), axis=0)), "rows", 0, 0),
+            axis=1,
+        )
         current = lax.psum_scatter(contribution, "scales", scatter_dimension=0, tiled=True)
     return current
 

time: 674 us -> 674 us (level)
  no operation moved by 1% of the time
where the time goes in v1:
time: 674 us; the launch traced here: 673 us
  blocking collectives  196 us (29%)
  waiting for transfers between devices  195 us (29%)
  other arithmetic  156 us (23%)
  starting transfers between devices  56.1 us (8%)
  local copies, waits for them, and re-layouts  49.7 us (7%)
  between operations  17.7 us (3%)
    psum x2, blocking collectives, body(): lax.psum((jnp.sum(descent * descent), jnp.sum(hessian_weight * blurred *...  89.8 us
    add x64, other arithmetic, forward_add_tap_row(): summed + tap_weights[:, column:column + 1] * shifted[:, column:column + c...  81 us
    all_to_all x2, blocking collectives, body(): lax.all_to_all(jnp.stack(jnp.split(kept, lax.axis_size('rows'), axis=0)),...  60.3 us
    all_to_all x2, waiting for transfers between devices, body(): lax.all_to_all(upper, 'rows', split_axis=1, concat_axis=0, tiled=True)  50.2 us
    reduce_scatter x2, waiting for transfers between devices, body(): lax.psum_scatter(contribution, 'scales', scatter_dimension=0, tiled=True)  49.5 us
    all_to_all x2, waiting for transfers between devices, body(): lax.all_to_all(lower, 'rows', split_axis=1, concat_axis=0, tiled=True)  48.3 us
    all_gather x1, blocking collectives, body(): tiles_in = lax.all_gather(psf_tiles, ('rows', 'scales'), axis=0, tiled=True)  45.4 us
    add x32, other arithmetic, adjoint_add_tap_row(): summed + tap_weights[:, column:column + 1] * shifted[:, offset_col:offset...  43.6 us
  transfers between devices with their start and end apart: 22, of which 13 were waited for; matrix products, arithmetic and copies ran while one was open for 1% of the time, Pallas kernels for 0%

profile of v1, /device:TPU:0, one launch (start us, length us, event | category | flops | bytes accessed | tf_op | source)
XLA Modules:
  0.0 673.3 jit_solution(17113526929602176010)
XLA Ops:
  7.6 2.4 collective-permute-start.2
  12.2 45.4 %all-gather = f32[32,1,256]{2,1,0:T(1,128)S(1)} all-gather(f32[1,1,256]{2,1,0:T(1,128)} %bitcast.139), channel_id=1, replica_groups=mesh['rows'=8,'scales'=4] {'rows','scales'}, dimensions={0}, use_global_device_ids=true | all-gather | bytes 33792 | tf_op jit(solution)/shard_map/all_gather | solution.py:105
  58.2 27.8 %while.146 = (s32[]{:T(128)}, f32[8,8192]{1,0:T(8,128)S(1)}, f32[8,16,16]{2,0,1:T(8,128)S(1)}, f32[24,8208]{1,0:T(8,128)S(1)}, s32[]{:T(128)}, /*index=5*/s32[]{...) while((s32[]{:T(128)}, f32[8,8192]{1,0:T(8,128)S(1)}, ...), condition=%wide.region_2.3_spmd.clone, body=%wide.region_1.2_spmd.clone.sunk | while | flops 2162706 | bytes 4721599 | solution.py:71
  89.7 3.0 collective-permute-start
  94.0 2.5 collective-permute-done.1
  97.0 29.6 %while.147 = (s32[]{:T(128)}, f32[8,8192]{1,0:T(8,128)S(1)}, f32[24,16,16]{2,0,1:T(8,128)S(1)}, f32[24,8208]{1,0:T(8,128)S(1)}, s32[]{:T(128)}, /*index=5*/s32[]...) while((s32[]{:T(128)}, f32[8,8192]{1,0:T(8,128)S(1)}, ...), condition=%wide.region_4.5_spmd.clone, body=%wide.region_3.4_spmd.clone.sunk | while | flops 2162713 | bytes 4721729 | solution.py:93
  127.3 4.3 collective-permute-start.6
  135.3 27.8 %while.148 = (s32[]{:T(128)}, f32[8,8192]{1,0:T(8,128)S(1)}, f32[8,16,16]{2,0,1:T(8,128)S(1)}, f32[24,8208]{1,0:T(8,128)S(1)}, s32[]{:T(128)}, /*index=5*/s32[]{...) while((s32[]{:T(128)}, f32[8,8192]{1,0:T(8,128)S(1)}, ...), condition=%wide.region_8.9_spmd.clone, body=%wide.region_7.8_spmd.clone.sunk | while | flops 2162706 | bytes 4721599 | solution.py:71
  163.9 42.4 %all-reduce.19 = (f32[]{:T(128)}, f32[]{:T(128)}) all-reduce(f32[]{:T(128)} %get-tuple-element.1221, f32[]{:T(128)} %fusion.137), channel_id=1, replica_groups=mesh['rows'=8,'scales'=4] {'rows','scales'}, use_global_device_ids=true, to_apply=%region_6.7 | all-reduce | flops 2 | bytes 16 | tf_op jit(solution)/shard_map/psum | solution.py:128
  208.5 17.4 %all-gather.4.cloned.1.call-done = f32[32,8192]{1,0:T(8,128)} async-done(((f32[8,8192]{1,0:T(8,128)}), f32[32,8192]{1,0:T(8,128)}) %all-gather.4.cloned.1.call-update) | async-done | bytes 1048592 | tf_op jit(solution)/shard_map/all_gather | solution.py:134
  225.8 4.2 multiply_add_fusion.5
  236.8 5.5 all-to-all-start.1
  243.4 25.1 %all-to-all-done.1 = f32[32,8,1024]{2,0,1:T(8,128)S(1)} async-done(((f32[32,8,1024]{2,0,1:T(8,128)}), f32[32,8,1024]{2,0,1:T(8,128)S(1)}, u32[]{:S(2)}, u32[]{:S(2)}) %all-to-all-start.1) | async-done | bytes 1048608 | tf_op jit(solution)/shard_map/all_to_all | solution.py:146
  268.5 3.8 all-to-all-start
  274.4 23.8 %all-to-all-done = f32[32,8,1024]{2,0,1:T(8,128)S(1)} async-done(((f32[32,8,1024]{2,0,1:T(8,128)}), f32[32,8,1024]{2,0,1:T(8,128)S(1)}, u32[]{:S(2)}, u32[]{:S(2)}) %all-to-all-start) | async-done | bytes 1048608 | tf_op jit(solution)/shard_map/all_to_all | solution.py:145
  298.7 30.1 %all_to_all.86 = f32[8,32,1024]{2,1,0:T(8,128)S(1)} all-to-all(f32[8,32,1024]{2,1,0:T(8,128)S(1)} %fusion.147), channel_id=1, replica_groups=mesh['rows'=8,'scales'=4] {'rows'}, dimensions={0} | all-to-all | bytes 2097152 | tf_op jit(solution)/shard_map/all_to_all | solution.py:157
  330.0 24.7 %reduce-scatter.3.cloned.1.call-done = f32[8,8192]{1,0:T(8,128)} async-done(((f32[32,8192]{1,0:T(8,128)}), f32[8,8192]{1,0:T(8,128)}) %reduce-scatter.3.cloned.1.call-update) | async-done | bytes 262160 | tf_op jit(solution)/shard_map/reduce_scatter | solution.py:160
  358.6 2.4 collective-permute-done.9
  361.3 27.8 %while.149 = (s32[]{:T(128)}, f32[8,8192]{1,0:T(8,128)S(1)}, f32[8,16,16]{2,0,1:T(8,128)S(1)}, f32[24,8208]{1,0:T(8,128)S(1)}, s32[]{:T(128)}, /*index=5*/s32[]{...) while((s32[]{:T(128)}, f32[8,8192]{1,0:T(8,128)S(1)}, ...), condition=%wide.region_18.19_spmd.clone, body=%wide.region_17.18_spmd.clone.sunk | while | flops 2162706 | bytes 4721599 | solution.py:71
  389.2 6.7 collective-permute-start.10
  399.8 29.6 %while.150 = (s32[]{:T(128)}, f32[8,8192]{1,0:T(8,128)S(1)}, f32[24,16,16]{2,0,1:T(8,128)S(1)}, f32[24,8208]{1,0:T(8,128)S(1)}, s32[]{:T(128)}, /*index=5*/s32[]...) while((s32[]{:T(128)}, f32[8,8192]{1,0:T(8,128)S(1)}, ...), condition=%wide.region_20.21_spmd.clone, body=%wide.region_19.20_spmd.clone.sunk | while | flops 2162713 | bytes 4721729 | solution.py:93
  430.0 8.0 %collective-permute-start.12 = (f32[8,8192]{1,0:T(8,128)S(1)}, f32[8,8192]{1,0:T(8,128)S(1)}, u32[]{:S(2)}, u32[]{:S(2)}) collective-permute-start(f32[8,8192]{1,0:T(8,128)S(1)} %get-tuple-element.1218), channel_id=1, source_target_pairs={{0,1},{1,2},{2,3},{3,4},{4,5},{5,6},{6,7},{7,8},{8,9},{9,10},{10,1... | collective-permute-start | bytes 786440 | tf_op jit(solution)/shard_map/ppermute | solution.py:21
  441.8 27.8 %while.151 = (s32[]{:T(128)}, f32[8,8192]{1,0:T(8,128)S(1)}, f32[8,16,16]{2,0,1:T(8,128)S(1)}, f32[24,8208]{1,0:T(8,128)S(1)}, s32[]{:T(128)}, /*index=5*/s32[]{...) while((s32[]{:T(128)}, f32[8,8192]{1,0:T(8,128)S(1)}, ...), condition=%wide.region_24.25_spmd.clone, body=%wide.region_23.24_spmd.clone.sunk | while | flops 2162706 | bytes 4721599 | solution.py:71
  470.3 47.3 %all-reduce.18 = (f32[]{:T(128)}, f32[]{:T(128)}) all-reduce(f32[]{:T(128)} %get-tuple-element.1217, f32[]{:T(128)} %fusion.138), channel_id=1, replica_groups=mesh['rows'=8,'scales'=4] {'rows','scales'}, use_global_device_ids=true, to_apply=%region_22.23 | all-reduce | flops 2 | bytes 16 | tf_op jit(solution)/shard_map/psum | solution.py:128
  519.7 18.3 %all-gather.6.cloned.1.call-done = f32[32,8192]{1,0:T(8,128)} async-done(((f32[8,8192]{1,0:T(8,128)}), f32[32,8192]{1,0:T(8,128)}) %all-gather.6.cloned.1.call-update) | async-done | bytes 1048592 | tf_op jit(solution)/shard_map/all_gather | solution.py:134
  538.0 4.2 multiply_add_fusion.2
  549.0 5.5 all-to-all-start.4
  555.5 25.1 %all-to-all-done.4 = f32[32,8,1024]{2,0,1:T(8,128)S(1)} async-done(((f32[32,8,1024]{2,0,1:T(8,128)}), f32[32,8,1024]{2,0,1:T(8,128)S(1)}, u32[]{:S(2)}, u32[]{:S(2)}) %all-to-all-start.4) | async-done | bytes 1048608 | tf_op jit(solution)/shard_map/all_to_all | solution.py:146
  580.6 3.6 all-to-all-start.3
  585.8 24.4 %all-to-all-done.3 = f32[32,8,1024]{2,0,1:T(8,128)S(1)} async-done(((f32[32,8,1024]{2,0,1:T(8,128)}), f32[32,8,1024]{2,0,1:T(8,128)S(1)}, u32[]{:S(2)}, u32[]{:S(2)}) %all-to-all-start.3) | async-done | bytes 1048608 | tf_op jit(solution)/shard_map/all_to_all | solution.py:145
  610.7 30.1 %all_to_all.87 = f32[8,32,1024]{2,1,0:T(8,128)S(1)} all-to-all(f32[8,32,1024]{2,1,0:T(8,128)S(1)} %fusion.139), channel_id=1, replica_groups=mesh['rows'=8,'scales'=4] {'rows'}, dimensions={0} | all-to-all | bytes 2097152 | tf_op jit(solution)/shard_map/all_to_all | solution.py:157
  641.9 24.8 %reduce-scatter.5.cloned.1.call-done = f32[8,8192]{1,0:T(8,128)} async-done(((f32[32,8192]{1,0:T(8,128)}), f32[8,8192]{1,0:T(8,128)}) %reduce-scatter.5.cloned.1.call-update) | async-done | bytes 262160 | tf_op jit(solution)/shard_map/reduce_scatter | solution.py:160
  (399 shorter events, 218.5 us)
Async XLA Ops:
  6.5 219.3 %all-gather.4.cloned.1.call-start = ((), (), s32[]{:S(2)}) async-start(), calls=%async_computation.8 | async-start | bytes 1310720 | tf_op jit(solution)/shard_map/all_gather | solution.py:134
  7.6 50.3 %collective-permute-start.2 = (f32[8,8192]{1,0:T(8,128)S(1)}, f32[8,8192]{1,0:T(8,128)S(1)}, u32[]{:S(2)}, u32[]{:S(2)}) collective-permute-start(f32[8,8192]{1,0:T(8,128)S(1)} %sub.46), channel_id=1, source_target_pairs={{0,1},{1,2},{2,3},{3,4},{4,5},{5,6},{6,7},{7,8},{8,9},{9,10},{10,1... | collective-permute-start | bytes 786440 | tf_op jit(solution)/shard_map/ppermute | solution.py:21
  10.0 47.9 %collective-permute-start.3 = (f32[8,8192]{1,0:T(8,128)S(1)}, f32[8,8192]{1,0:T(8,128)S(1)}, u32[]{:S(2)}, u32[]{:S(2)}) collective-permute-start(f32[8,8192]{1,0:T(8,128)S(1)} %sub.46), channel_id=1, source_target_pairs={{1,0},{2,1},{3,2},{4,3},{5,4},{6,5},{7,6},{8,7},{9,8},{10,9},{11,1... | collective-permute-start | bytes 786440 | tf_op jit(solution)/shard_map/ppermute | solution.py:23
  58.2 27.8 %copy-start = (f32[8,8192]{1,0:T(8,128)S(1)}, f32[8,8192]{1,0:T(8,128)}, u32[]{:S(2)}) copy-start(f32[8,8192]{1,0:T(8,128)} %param.29) | copy-start | bytes 786436
  86.1 10.6 %collective-permute-start.4 = (f32[8,8192]{1,0:T(8,128)S(1)}, f32[8,8192]{1,0:T(8,128)S(1)}, u32[]{:S(2)}, u32[]{:S(2)}) collective-permute-start(f32[8,8192]{1,0:T(8,128)S(1)} %mul.2942), channel_id=1, source_target_pairs={{0,1},{1,2},{2,3},{3,4},{4,5},{5,6},{6,7},{7,8},{8,9},{9,10},{10,1... | collective-permute-start | bytes 786440 | tf_op jit(solution)/shard_map/ppermute | solution.py:21
  88.4 8.4 %collective-permute-start.5 = (f32[8,8192]{1,0:T(8,128)S(1)}, f32[8,8192]{1,0:T(8,128)S(1)}, u32[]{:S(2)}, u32[]{:S(2)}) collective-permute-start(f32[8,8192]{1,0:T(8,128)S(1)} %mul.2942), channel_id=1, source_target_pairs={{1,0},{2,1},{3,2},{4,3},{5,4},{6,5},{7,6},{8,7},{9,8},{10,9},{11,1... | collective-permute-start | bytes 786440 | tf_op jit(solution)/shard_map/ppermute | solution.py:23
  89.7 4.4 collective-permute-start
  92.7 3.8 collective-permute-start.1
  97.0 29.6 %copy-start.5 = (f32[8,8192]{1,0:T(8,128)S(1)}, f32[8,8192]{1,0:T(8,128)}, u32[]{:S(2)}) copy-start(f32[8,8192]{1,0:T(8,128)} %param.28) | copy-start | bytes 786436
  127.3 5.6 collective-permute-start.6
  131.6 3.4 collective-permute-start.7
  135.3 72.4 %copy-start.1 = (f32[8,8192]{1,0:T(8,128)S(1)}, f32[8,8192]{1,0:T(8,128)}, u32[]{:S(2)}) copy-start(f32[8,8192]{1,0:T(8,128)} %param.27) | copy-start | bytes 786436
  230.0 1.2 copy-start.2
  236.8 31.7 %all-to-all-start.1 = ((f32[32,8,1024]{2,0,1:T(8,128)}), f32[32,8,1024]{2,0,1:T(8,128)S(1)}, u32[]{:S(2)}, u32[]{:S(2)}) async-start(f32[32,8,1024]{2,0,1:T(8,128)} %bitcast.112), calls=%async_computation.1 | async-start | bytes 2097152 | tf_op jit(solution)/shard_map/all_to_all | solution.py:146
  268.5 3.8 copy-start.6
  268.5 29.7 %all-to-all-start = ((f32[32,8,1024]{2,0,1:T(8,128)}), f32[32,8,1024]{2,0,1:T(8,128)S(1)}, u32[]{:S(2)}, u32[]{:S(2)}) async-start(f32[32,8,1024]{2,0,1:T(8,128)} %bitcast.130), calls=%async_computation | async-start | bytes 2097152 | tf_op jit(solution)/shard_map/all_to_all | solution.py:145
  272.3 82.5 %reduce-scatter.3.cloned.1.call-start = ((), (), s32[]{:S(2)}) async-start(), calls=%async_computation.9 | async-start | bytes 1310720 | tf_op jit(solution)/shard_map/reduce_scatter | solution.py:160
  330.0 208.0 %all-gather.6.cloned.1.call-start = ((), (), s32[]{:S(2)}) async-start(), calls=%async_computation.10 | async-start | bytes 1310720 | tf_op jit(solution)/shard_map/all_gather | solution.py:134
  355.7 2.9 collective-permute-start.8
  357.3 3.7 collective-permute-start.9
  389.2 8.2 %collective-permute-start.10 = (f32[8,8192]{1,0:T(8,128)S(1)}, f32[8,8192]{1,0:T(8,128)S(1)}, u32[]{:S(2)}, u32[]{:S(2)}) collective-permute-start(f32[8,8192]{1,0:T(8,128)S(1)} %mul.2961), channel_id=1, source_target_pairs={{0,1},{1,2},{2,3},{3,4},{4,5},{5,6},{6,7},{7,8},{8,9},{9,10},{10,1... | collective-permute-start | bytes 786440 | tf_op jit(solution)/shard_map/ppermute | solution.py:21
  395.8 3.6 collective-permute-start.11
  430.0 9.4 %collective-permute-start.12 = (f32[8,8192]{1,0:T(8,128)S(1)}, f32[8,8192]{1,0:T(8,128)S(1)}, u32[]{:S(2)}, u32[]{:S(2)}) collective-permute-start(f32[8,8192]{1,0:T(8,128)S(1)} %get-tuple-element.1218), channel_id=1, source_target_pairs={{0,1},{1,2},{2,3},{3,4},{4,5},{5,6},{6,7},{7,8},{8,9},{9,10},{10,1... | collective-permute-start | bytes 786440 | tf_op jit(solution)/shard_map/ppermute | solution.py:21
  438.1 3.4 collective-permute-start.13
  441.8 77.2 %copy-start.4 = (f32[8,8192]{1,0:T(8,128)S(1)}, f32[8,8192]{1,0:T(8,128)}, u32[]{:S(2)}) copy-start(f32[8,8192]{1,0:T(8,128)} %reduce-scatter.3.cloned.1.call-done) | copy-start | bytes 786436
  542.2 1.2 copy-start.3
  549.0 31.7 %all-to-all-start.4 = ((f32[32,8,1024]{2,0,1:T(8,128)}), f32[32,8,1024]{2,0,1:T(8,128)S(1)}, u32[]{:S(2)}, u32[]{:S(2)}) async-start(f32[32,8,1024]{2,0,1:T(8,128)} %bitcast.110), calls=%async_computation.5 | async-start | bytes 2097152 | tf_op jit(solution)/shard_map/all_to_all | solution.py:146
  580.6 29.6 %all-to-all-start.3 = ((f32[32,8,1024]{2,0,1:T(8,128)}), f32[32,8,1024]{2,0,1:T(8,128)S(1)}, u32[]{:S(2)}, u32[]{:S(2)}) async-start(f32[32,8,1024]{2,0,1:T(8,128)} %bitcast.111), calls=%async_computation.4 | async-start | bytes 2097152 | tf_op jit(solution)/shard_map/all_to_all | solution.py:145
  584.3 82.5 %reduce-scatter.5.cloned.1.call-start = ((), (), s32[]{:S(2)}) async-start(), calls=%async_computation.11 | async-start | bytes 1310720 | tf_op jit(solution)/shard_map/reduce_scatter | solution.py:160
Sparse Core Ops, SparseCore 0:
  208.6 17.2 all-gather.3
  330.1 24.6 reduce-scatter.2
  519.9 18.0 all-gather.5
  642.1 24.6 reduce-scatter.4
